TPU v7x, 32 devices: a whole 2x2x4 slice. The times are simulated.
32 devices in a mesh: row: 4 (over x, core), col: 8 (over z, y).
Axes of the slice: x: 2, y: 2, z: 4, core: 2. Of those that a mesh axis runs over, the one named last changes fastest.
Arguments:
- signatures: bfloat16 [2048, 49152], P('row', 'col'), as said below
- trailing: float32 [2048, 1024], P('row', 'col'), may hold values from -6 to 6
- ridge: float32 [1], replicated, may hold values from 0.5 to 2
- panel_index: int32 [1], replicated, may hold values from 1 to 3
Outputs:
- factor: float32 [2048, 256], P(('row', 'col'))
- updated: float32 [2048, 1024], P('row', 'col')
Inputs may be any that keep to these rules, and one draw needn't show every extreme that they name: `signatures`: every diagonal block of the Gram matrix plus the ridge is positive definite.
All inputs are finite; a program needn't handle non-finite values.
Results may differ from a plain program's by a relative error of at most 0.0003.
Values may be sent and summed in bfloat16 or wider, within the bound.
A program may use at most 64 MiB of HBM per device.

v0:
```python
import jax
import jax.numpy as jnp
from jax import lax
from jax.sharding import PartitionSpec as P

PANEL = 256


def spread(block, axis, owner):
    block = jnp.where(lax.axis_index(axis) == owner, block, jnp.zeros_like(block))
    return lax.psum(block, axis)


def add_ridge(block, first_row, panel_start, ridge):
    row_ids = first_row + lax.broadcasted_iota(jnp.int32, block.shape, 0)
    col_ids = panel_start + lax.broadcasted_iota(jnp.int32, block.shape, 1)
    return block + jnp.where(row_ids == col_ids, ridge[0], jnp.zeros((), block.dtype))


def mask_above(block, first_row, panel_start):
    row_ids = first_row + lax.broadcasted_iota(jnp.int32, block.shape, 0)
    return jnp.where(row_ids >= panel_start, block, jnp.zeros((), block.dtype))


def solve_rows(lower, panel_rows):
    return jax.scipy.linalg.solve_triangular(lower, panel_rows.T, lower=True).T


def local(signatures, trailing, ridge, panel_index):
    rows_dev = signatures.shape[0]
    tile_cols = trailing.shape[1]
    col_count = lax.axis_size("col")
    row_share = rows_dev // col_count
    row_pos = lax.axis_index("row")
    col_pos = lax.axis_index("col")
    panel_start = panel_index[0] * PANEL
    row_owner = panel_start // rows_dev
    local_offset = panel_start % rows_dev
    own_paths = lax.dynamic_slice_in_dim(signatures, local_offset, PANEL, 0)
    panel_paths = spread(own_paths, "row", row_owner)
    mine_rows = lax.psum_scatter(
        lax.dot_general(
            signatures, panel_paths, (((1,), (1,)), ((), ())), preferred_element_type=jnp.float32
        ),
        "col",
        scatter_dimension=0,
        tiled=True,
    )
    mine_rows = add_ridge(mine_rows, row_pos * rows_dev + col_pos * row_share, panel_start, ridge)
    own_block = lax.dot_general(
        panel_paths, panel_paths, (((1,), (1,)), ((), ())), preferred_element_type=jnp.float32
    )
    diagonal = lax.psum(own_block, "col")
    diagonal = add_ridge(diagonal, panel_start, panel_start, ridge)
    lower = jnp.linalg.cholesky(diagonal)
    factor_mine = solve_rows(lower, mine_rows)
    factor_mine = mask_above(factor_mine, row_pos * rows_dev + col_pos * row_share, panel_start)
    factor_block = lax.all_gather(factor_mine, "col", axis=0, tiled=True)
    window_start = panel_start + PANEL + col_pos * tile_cols
    window_owner = window_start // rows_dev
    window_cut = lax.dynamic_slice_in_dim(factor_block, window_start % rows_dev, tile_cols, 0)
    window_rows = spread(window_cut, "row", window_owner)
    updated = trailing - lax.dot_general(
        factor_block,
        window_rows,
        (((1,), (1,)), ((), ())),
        precision=lax.Precision.HIGHEST,
        preferred_element_type=jnp.float32,
    )
    return (factor_mine, updated)


def solution(mesh):
    placed = (P("row", "col"), P("row", "col"), P(), P())
    return jax.shard_map(
        local,
        mesh=mesh,
        in_specs=placed,
        out_specs=(P(("row", "col"), None), P("row", "col")),
        check_vma=False,
    )
```

profile of v0, /device:TPU:0, one launch (start us, length us, event | category | flops | bytes accessed | tf_op | source)
XLA Modules:
  0.0 299.6 jit_solution(7277814875881397498)
XLA Ops:
  7.2 0.0 all-reduce.5.cloned.1.call-start
  7.9 4.5 %dynamic-slice_select_fusion = bf16[256,6144]{1,0:T(8,128)(2,1)} fusion(bf16[512,6144]{1,0:T(8,128)(2,1)} %param.4, s32[]{:T(128)S(6)} %select_n.62, pred[]{:T(512)S(6)} %eq.15), kind=kLoop, calls=%fused_computation.2 | loop fusion | flops 1572864 | bytes 6291461 | tf_op jit(solution)/shard_map/jit(_where)/select_n | solution.py:10
  12.4 0.0 all-reduce.5.cloned.1.call-update
  12.5 0.0 all-reduce.7.cloned.1.call-start
  13.3 70.5 %all-reduce.5.cloned.1.call-done = bf16[256,6144]{1,0:T(8,128)(2,1)} async-done(((bf16[256,6144]{1,0:T(8,128)(2,1)}), bf16[256,6144]{1,0:T(8,128)(2,1)}) %all-reduce.5.cloned.1.call-update) | async-done | bytes 3145744 | tf_op jit(solution)/shard_map/psum | solution.py:11
  83.8 4.6 %fusion.10 = f32[256,256]{0,1:T(8,128)} fusion(bf16[256,6144]{1,0:T(8,128)(2,1)} %all-reduce.5.cloned.1.call-done), kind=kOutput, calls=%fused_computation.39 | convolution fusion | flops 805306368 | bytes 3407872 | tf_op jit(solution)/shard_map/dot_general | solution.py:50
  88.3 0.0 all-reduce.7.cloned.1.call-update
  88.3 0.0 reduce-scatter.4.cloned.1.call-start
  88.4 5.6 %convolution_bitcast_fusion = f32[512,256]{0,1:T(8,128)S(1)} fusion(bf16[256,6144]{1,0:T(8,128)(2,1)} %all-reduce.5.cloned.1.call-done, bf16[512,6144]{1,0:T(8,128)(2,1)} %param.4), kind=kOutput, calls=%fused_computation.3 | convolution fusion | flops 1610612736 | bytes 9961472 | tf_op jit(solution)/shard_map/dot_general | solution.py:42
  94.0 1.0 copy.19
  95.0 0.0 reduce-scatter.4.cloned.1.call-update
  95.0 0.2 all-reduce.9.cloned.1.call-start
  95.2 64.4 %all-reduce.7.cloned.1.call-done = f32[256,256]{0,1:T(8,128)} async-done(((f32[256,256]{0,1:T(8,128)}), f32[256,256]{0,1:T(8,128)}) %all-reduce.7.cloned.1.call-update) | async-done | bytes 262160 | tf_op jit(solution)/shard_map/psum | solution.py:53
  159.6 1.0 select_add_fusion
  160.7 0.1 copy.13
  160.8 1.1 fusion
  161.9 11.7 %cholesky.49 = f32[128,128]{1,0:T(8,128)S(1)} custom-call(f32[128,128]{1,0:T(8,128)S(1)} %cholesky.115), custom_call_target="Cholesky" | custom-call | tf_op jit(solution)/shard_map/jit(cholesky)/cholesky | solution.py:55
  173.7 9.8 %custom-call.15 = f32[1,128,128]{1,2,0:T(8,128)S(1)} custom-call(f32[1,128,128]{2,1,0:T(8,128)S(1)} %get-tuple-element.29), custom_call_target="InvertDiagBlocksLowerTriangular" | custom-call | tf_op jit(solution)/shard_map/jit(cholesky)/cholesky | solution.py:55
  183.5 0.0 copy-start.1
  183.5 0.2 fusion.5
  183.7 0.3 convolution_subtract_fusion.2
  184.0 11.7 %cholesky.103 = f32[128,128]{1,0:T(8,128)S(1)} custom-call(f32[128,128]{1,0:T(8,128)S(1)} %convolution_subtract_fusion.2), custom_call_target="Cholesky" | custom-call | tf_op jit(solution)/shard_map/jit(cholesky)/cholesky | solution.py:55
  195.7 0.1 copy.16
  195.8 0.1 copy.15
  195.9 0.1 copy.14
  196.0 0.6 compare_reduce_fusion
  198.1 0.1 triangular_solve.60
  198.1 4.4 %while.1 = (s32[]{:T(128)}, f32[256,256]{0,1:T(8,128)S(1)}, s32[2,2]{1,0:T(2,128)S(1)}, f32[2,128,128]{2,1,0:T(8,128)S(1)}, s32[]{:T(128)}) while((s32[]{:T(128)}, f32[256,256]{0,1:T(8,128)S(1)}, s32[2,2]{1,0:T(2,128)S(1)}, f32[2,128,128]{2,1,0:T(8,128)S(1)}, s32[]{:T(128)}) %tuple.27), condition=%wide.while_cond, body=%wide.while_body.sunk | while | flops 2 | bytes 393321 | solution.py:26
  198.3 0.6 fusion.22
  198.9 1.4 dynamic-slice.7
  200.3 0.1 copy.23
  200.4 0.6 fusion.22
  201.0 1.4 dynamic-slice.7
  202.4 0.1 copy.23
  202.5 19.7 %custom-call.16 = f32[2,128,128]{1,2,0:T(8,128)S(1)} custom-call(f32[2,128,128]{2,1,0:T(8,128)S(1)} %get-tuple-element.9), custom_call_target="InvertDiagBlocksLowerTriangular" | custom-call | tf_op jit(solution)/shard_map/jit(_solve_triangular)/triangular_solve | solution.py:26
  222.2 3.6 %reduce-scatter.4.cloned.1.call-done = f32[64,256]{1,0:T(8,128)} async-done(((f32[512,256]{1,0:T(8,128)}), f32[64,256]{1,0:T(8,128)}) %reduce-scatter.4.cloned.1.call-update) | async-done | bytes 65552
  225.8 0.9 copy.20
  226.7 0.1 add_bitcast_fusion
  226.8 0.3 fusion.3
  227.1 0.3 convolution_subtract_fusion.1
  227.4 0.3 fusion.2
  227.7 0.1 fusion.7
  227.8 0.0 copy-start
  227.8 31.4 %all_gather.3 = f32[512,256]{1,0:T(8,128)S(1)} all-gather(f32[64,256]{1,0:T(8,128)S(1)} %fusion.7), channel_id=1, replica_groups=mesh['row'=4,'col'=8] {'col'}, dimensions={0}, use_global_device_ids=true | all-gather | bytes 589824 | tf_op jit(solution)/shard_map/all_gather | solution.py:58
  259.2 0.7 dynamic-slice_select_fusion.1
  259.9 0.0 all-reduce.9.cloned.1.call-update
  259.9 30.9 %all-reduce.9.cloned.1.call-done = f32[128,256]{1,0:T(8,128)} async-done(((f32[128,256]{1,0:T(8,128)}), f32[128,256]{1,0:T(8,128)}) %all-reduce.9.cloned.1.call-update) | async-done | bytes 131088 | tf_op jit(solution)/shard_map/psum | solution.py:11
  290.8 0.0 copy-done.1
  290.9 2.2 convolution_subtract_fusion
  293.0 0.0 copy-done
  (16 shorter events, 0.2 us)
Async XLA Ops:
  7.2 76.6 %all-reduce.5.cloned.1.call-start = ((), (), s32[]{:S(2)}) async-start(), calls=%async_computation.1 | async-start | bytes 6291456 | tf_op jit(solution)/shard_map/psum | solution.py:11
  12.5 147.2 %all-reduce.7.cloned.1.call-start = ((), (), s32[]{:S(2)}) async-start(), calls=%async_computation.2 | async-start | bytes 524288 | tf_op jit(solution)/shard_map/psum | solution.py:53
  88.3 137.4 %reduce-scatter.4.cloned.1.call-start = ((), (), s32[]{:S(2)}) async-start(), calls=%async_computation.4 | async-start | bytes 589824
  95.0 195.9 %all-reduce.9.cloned.1.call-start = ((), (), s32[]{:S(2)}) async-start(), calls=%async_computation.3 | async-start | bytes 262144 | tf_op jit(solution)/shard_map/psum | solution.py:11
  183.5 107.4 %copy-start.1 = (f32[512,128]{1,0:T(8,128)S(1)}, f32[512,128]{1,0:T(8,128)}, u32[]{:S(2)}) copy-start(f32[512,128]{1,0:T(8,128)} %param.5) | copy-start | bytes 786436
  227.8 65.3 %copy-start = (f32[64,256]{1,0:T(8,128)}, f32[64,256]{1,0:T(8,128)S(1)}, u32[]{:S(2)}) copy-start(f32[64,256]{1,0:T(8,128)S(1)} %fusion.7) | copy-start | bytes 196612
Sparse Core Ops, SparseCore 0:
  12.6 71.1 all-reduce.4
  88.5 71.1 all-reduce.6
  163.0 62.7 reduce-scatter.3
  260.0 30.7 all-reduce.8
where the time goes:
time: 300 us
  waiting for transfers between devices  169 us (56%)
  other arithmetic  61.2 us (20%)
  blocking collectives  31.4 us (10%)
  between operations  16.7 us (6%)
  matrix products  13.6 us (5%)
  local copies, waits for them, and re-layouts  6.6 us (2%)
    psum x2, waiting for transfers between devices, spread(): return lax.psum(block, axis)  101 us
    psum x1, waiting for transfers between devices, local(): diagonal = lax.psum(own_block, 'col')  64.4 us
    another operation x6, other arithmetic, local(): lower = jnp.linalg.cholesky(diagonal)  34 us
    all_gather x1, blocking collectives, local(): factor_block = lax.all_gather(factor_mine, 'col', axis=0, tiled=True)  31.4 us
    another operation x3, other arithmetic, solve_rows(): return jax.scipy.linalg.solve_triangular(lower, panel_rows.T, lower=True).T  19.7 us
  transfers between devices with their start and end apart: 4, of which 4 were waited for; matrix products, arithmetic and copies ran while one was open for 23% of the time, Pallas kernels for 0%

commit v1 on v0

--- a/solution.py
+++ b/solution.py
@@ -50,7 +50,7 @@
     own_block = lax.dot_general(
         panel_paths, panel_paths, (((1,), (1,)), ((), ())), preferred_element_type=jnp.float32
     )
-    diagonal = lax.psum(own_block, "col")
+    diagonal = jax.lax.all_gather(own_block, "col").sum(axis=0)
     diagonal = add_ridge(diagonal, panel_start, panel_start, ridge)
     lower = jnp.linalg.cholesky(diagonal)
     factor_mine = solve_rows(lower, mine_rows)

time: 300 us -> 338 us (1.13)
  waiting for transfers between devices: 169 us -> 209 us
    psum x1 -> x0, waiting for transfers between devices: 64.4 us -> none  [local(): diagonal = lax.psum(own_block, 'col')]
    unnamed x5, waiting for transfers between devices: 3.63 us -> 57.3 us
    all_gather x0 -> x1, waiting for transfers between devices: none -> 49.7 us  [local(): diagonal = jax.lax.all_gather(own_block, 'col').sum(axis=0)]
  transfers between devices with their start and end apart: 4 -> 4, of which waited for: 4 -> 4; matrix products, arithmetic and copies ran while one was open for 23% -> 2% of each run, Pallas kernels for 0% -> 0%
where the time goes in v1:
time: 338 us
  waiting for transfers between devices  209 us (62%)
  other arithmetic  61 us (18%)
  blocking collectives  31.4 us (9%)
  between operations  16.6 us (5%)
  matrix products  13.5 us (4%)
  local copies, waits for them, and re-layouts  6.11 us (2%)
    psum x2, waiting for transfers between devices, spread(): return lax.psum(block, axis)  102 us
    unnamed x5, waiting for transfers between devices  57.3 us
    all_gather x1, waiting for transfers between devices, local(): diagonal = jax.lax.all_gather(own_block, 'col').sum(axis=0)  49.7 us
    another operation x6, other arithmetic, local(): lower = jnp.linalg.cholesky(diagonal)  33.9 us
    all_gather x1, blocking collectives, local(): factor_block = lax.all_gather(factor_mine, 'col', axis=0, tiled=True)  31.4 us
    another operation x3, other arithmetic, solve_rows(): return jax.scipy.linalg.solve_triangular(lower, panel_rows.T, lower=True).T  19.7 us
  transfers between devices with their start and end apart: 4, of which 4 were waited for; matrix products, arithmetic and copies ran while one was open for 2% of the time, Pallas kernels for 0%

profile of v1, /device:TPU:0, one launch (start us, length us, event | category | flops | bytes accessed | tf_op | source)
XLA Modules:
  0.0 337.9 jit_solution(7236050195148766943)
XLA Ops:
  7.2 0.0 all-reduce.4.cloned.1.call-start
  7.9 4.5 %dynamic-slice_select_fusion = bf16[256,6144]{1,0:T(8,128)(2,1)} fusion(bf16[512,6144]{1,0:T(8,128)(2,1)} %param.4, s32[]{:T(128)S(6)} %select_n.65, pred[]{:T(512)S(6)} %eq.18), kind=kLoop, calls=%fused_computation.2 | loop fusion | flops 1572864 | bytes 6291461 | tf_op jit(solution)/shard_map/jit(_where)/select_n | solution.py:10
  12.4 0.0 all-reduce.4.cloned.1.call-update
  12.5 0.0 reduce-scatter.4.cloned.1.call-start
  12.5 71.3 %all-reduce.4.cloned.1.call-done = bf16[256,6144]{1,0:T(8,128)(2,1)} async-done(((bf16[256,6144]{1,0:T(8,128)(2,1)}), bf16[256,6144]{1,0:T(8,128)(2,1)}) %all-reduce.4.cloned.1.call-update) | async-done | bytes 3145744 | tf_op jit(solution)/shard_map/psum | solution.py:11
  83.8 5.6 %convolution_bitcast_fusion = f32[512,256]{0,1:T(8,128)S(1)} fusion(bf16[256,6144]{1,0:T(8,128)(2,1)} %all-reduce.4.cloned.1.call-done, bf16[512,6144]{1,0:T(8,128)(2,1)} %param.4), kind=kOutput, calls=%fused_computation.3 | convolution fusion | flops 1610612736 | bytes 9961472 | tf_op jit(solution)/shard_map/dot_general | solution.py:42
  89.3 1.0 copy.8
  90.3 0.0 reduce-scatter.4.cloned.1.call-update
  90.4 0.0 all-gather.3.cloned.1.call-start
  90.4 4.6 %fusion.9 = f32[256,256]{1,0:T(8,128)} fusion(bf16[256,6144]{1,0:T(8,128)(2,1)} %all-reduce.4.cloned.1.call-done), kind=kOutput, calls=%fused_computation.37 | convolution fusion | flops 805306368 | bytes 3407872 | tf_op jit(solution)/shard_map/dot_general | solution.py:50
  95.0 0.0 all-gather.3.cloned.1.call-update
  95.0 0.2 all-reduce.6.cloned.1.call-start
  96.0 57.3 %reduce-scatter.4.cloned.1.call-done = f32[64,256]{1,0:T(8,128)} async-done(((f32[512,256]{1,0:T(8,128)}), f32[64,256]{1,0:T(8,128)}) %reduce-scatter.4.cloned.1.call-update) | async-done | bytes 65552
  153.3 0.9 copy.9
  154.2 0.1 add_bitcast_fusion
  154.3 49.7 %all-gather.3.cloned.1.call-done = f32[2048,256]{1,0:T(8,128)} async-done(((f32[256,256]{1,0:T(8,128)}), f32[2048,256]{1,0:T(8,128)}) %all-gather.3.cloned.1.call-update) | async-done | bytes 2097168 | tf_op jit(solution)/shard_map/all_gather | solution.py:53
  204.0 1.8 reduce_sum.11
  205.8 0.0 copy-start.1
  205.8 0.1 copy.7
  206.0 0.1 add_multiply_fusion
  206.1 11.7 %cholesky.49 = f32[128,128]{1,0:T(8,128)S(1)} custom-call(f32[128,128]{1,0:T(8,128)S(1)} %cholesky.115), custom_call_target="Cholesky" | custom-call | tf_op jit(solution)/shard_map/jit(cholesky)/cholesky | solution.py:55
  217.9 9.8 %custom-call.15 = f32[1,128,128]{1,2,0:T(8,128)S(1)} custom-call(f32[1,128,128]{2,1,0:T(8,128)S(1)} %get-tuple-element.23), custom_call_target="InvertDiagBlocksLowerTriangular" | custom-call | tf_op jit(solution)/shard_map/jit(cholesky)/cholesky | solution.py:55
  227.7 0.2 constant_dynamic-update-slice_fusion
  227.9 0.3 convolution_subtract_fusion.2
  228.2 11.7 %cholesky.103 = f32[128,128]{1,0:T(8,128)S(1)} custom-call(f32[128,128]{1,0:T(8,128)S(1)} %convolution_subtract_fusion.2), custom_call_target="Cholesky" | custom-call | tf_op jit(solution)/shard_map/jit(cholesky)/cholesky | solution.py:55
  239.9 0.6 compare_reduce_fusion
  241.9 0.1 triangular_solve.60
  242.0 4.2 %while.1 = (s32[]{:T(128)}, f32[256,256]{1,0:T(8,128)S(1)}, s32[2,2]{1,0:T(2,128)S(1)}, f32[2,128,128]{2,1,0:T(8,128)S(1)}, s32[]{:T(128)}) while((s32[]{:T(128)}, f32[256,256]{1,0:T(8,128)S(1)}, s32[2,2]{1,0:T(2,128)S(1)}, f32[2,128,128]{2,1,0:T(8,128)S(1)}, s32[]{:T(128)}) %tuple.27), condition=%wide.while_cond, body=%wide.while_body.sunk | while | flops 2 | bytes 131181 | solution.py:26
  242.2 0.6 fusion.21
  242.8 1.4 bitcast_dynamic-update-slice_fusion.2
  244.2 0.6 fusion.21
  244.8 1.4 bitcast_dynamic-update-slice_fusion.2
  246.2 19.7 %custom-call.16 = f32[2,128,128]{1,2,0:T(8,128)S(1)} custom-call(f32[2,128,128]{2,1,0:T(8,128)S(1)} %get-tuple-element.9), custom_call_target="InvertDiagBlocksLowerTriangular" | custom-call | tf_op jit(solution)/shard_map/jit(_solve_triangular)/triangular_solve | solution.py:26
  265.8 0.3 fusion.2
  266.1 0.2 convolution_subtract_fusion.1
  266.3 0.3 fusion.1
  266.6 0.1 fusion.6
  266.7 0.0 copy-start
  266.7 31.4 %all_gather.11 = f32[512,256]{1,0:T(8,128)S(1)} all-gather(f32[64,256]{1,0:T(8,128)S(1)} %fusion.6), channel_id=1, replica_groups=mesh['row'=4,'col'=8] {'col'}, dimensions={0}, use_global_device_ids=true | all-gather | bytes 589824 | tf_op jit(solution)/shard_map/all_gather | solution.py:58
  298.1 0.7 dynamic-slice_select_fusion.1
  298.8 0.0 all-reduce.6.cloned.1.call-update
  298.8 30.4 %all-reduce.6.cloned.1.call-done = f32[128,256]{1,0:T(8,128)} async-done(((f32[128,256]{1,0:T(8,128)}), f32[128,256]{1,0:T(8,128)}) %all-reduce.6.cloned.1.call-update) | async-done | bytes 131088 | tf_op jit(solution)/shard_map/psum | solution.py:11
  329.2 0.0 copy-done.1
  329.2 2.2 convolution_subtract_fusion
  331.4 0.0 copy-done
  (12 shorter events, 0.2 us)
Async XLA Ops:
  7.2 76.6 %all-reduce.4.cloned.1.call-start = ((), (), s32[]{:S(2)}) async-start(), calls=%async_computation.1 | async-start | bytes 6291456 | tf_op jit(solution)/shard_map/psum | solution.py:11
  12.5 140.8 %reduce-scatter.4.cloned.1.call-start = ((), (), s32[]{:S(2)}) async-start(), calls=%async_computation.4 | async-start | bytes 589824
  90.4 113.7 %all-gather.3.cloned.1.call-start = ((), (), s32[]{:S(2)}) async-start(), calls=%async_computation.3 | async-start | bytes 2359296 | tf_op jit(solution)/shard_map/all_gather | solution.py:53
  95.0 234.2 %all-reduce.6.cloned.1.call-start = ((), (), s32[]{:S(2)}) async-start(), calls=%async_computation.2 | async-start | bytes 262144 | tf_op jit(solution)/shard_map/psum | solution.py:11
  205.8 123.4 %copy-start.1 = (f32[512,128]{1,0:T(8,128)S(1)}, f32[512,128]{1,0:T(8,128)}, u32[]{:S(2)}) copy-start(f32[512,128]{1,0:T(8,128)} %param.5) | copy-start | bytes 786436
  266.7 64.7 %copy-start = (f32[64,256]{1,0:T(8,128)}, f32[64,256]{1,0:T(8,128)S(1)}, u32[]{:S(2)}) copy-start(f32[64,256]{1,0:T(8,128)S(1)} %fusion.6) | copy-start | bytes 196612
Sparse Core Ops, SparseCore 0:
  12.6 71.1 all-reduce.3
  90.5 62.7 reduce-scatter.3
  156.0 48.0 all-gather.2
  298.9 30.2 all-reduce.5
